TPU v7x, 32 devices: a whole 2x2x4 slice. The times are simulated.
32 devices in a mesh: row: 4 (over x, core), col: 8 (over z, y).
Axes of the slice: x: 2, y: 2, z: 4, core: 2. Of those that a mesh axis runs over, the one named last changes fastest.
Arguments:
- hidden: bfloat16 [128, 8192], P('row', 'col'), may hold values from -6 to 6
- vectors: float32 [4, 8192], P(None, 'col'), may hold values from -6 to 6
- gain: float32 [8192], P('col'), may hold values from 0.25 to 1.75
- lengths: int32 [2], replicated, may hold values from 16 to 64, as said below
- gate_weight: bfloat16 [8192, 29568], P('col', 'row'), may hold values from -0.0625 to 0.0625
- up_weight: bfloat16 [8192, 29568], P('col', 'row'), may hold values from -0.0625 to 0.0625
- down_weight: bfloat16 [29568, 8192], P('row', 'col'), may hold values from -0.03125 to 0.03125
Outputs:
- output: bfloat16 [128, 8192], P('row', 'col')
- tangent_out: bfloat16 [128, 4, 8192], P('row', None, 'col')
- new_vectors: float32 [4, 8192], P(None, 'col')
- back_cross: float32 [128, 4], P('row')
Inputs may be any that keep to these rules, and one draw needn't show every extreme that they name: `lengths`: each prompt's live tokens come first; in every draw exactly one prompt has all 64 tokens live.
All inputs are finite; a program needn't handle non-finite values.
Results may differ from a plain program's by a relative error of at most 0.025.
Values may be sent and summed in bfloat16 or wider, within the bound.
No kernel may reach another device: no remote copies, remote signals or barrier semaphores. Data moves between devices by JAX's collectives and lax.ppermute only.
A program may use at most 192 MiB of HBM per device.

v0:
```python
import jax
import jax.numpy as jnp
from jax import lax
from jax.sharding import PartitionSpec as P

D = 8192
LEN = 64


EPSILON = 1e-06
HIGH = lax.Precision.HIGHEST


def silu_parts(value):
    sigmoid = jax.nn.sigmoid(value)
    return (value * sigmoid, sigmoid * (1.0 + value * (1.0 - sigmoid)))


def contract(left, right, left_dim, right_dim):
    return lax.dot_general(
        left, right, (((left_dim,), (right_dim,)), ((), ())), preferred_element_type=jnp.float32
    )


def per_device(hidden, vectors, gain, lengths, gate_weight, up_weight, down_weight):
    rows_row = hidden.shape[0]
    width_col = hidden.shape[1]
    count = vectors.shape[0]
    width_s = count + 1
    tokens = rows_row * lax.axis_size("row")
    hidden_f = hidden.astype(jnp.float32)
    square, cross = lax.psum(
        (jnp.sum(hidden_f * hidden_f, axis=1), jnp.dot(hidden_f, vectors.T, precision=HIGH)), "col"
    )
    rscale = lax.rsqrt(square / D + EPSILON)
    primal = hidden_f * rscale[:, None] * gain
    tangent = (
        vectors[None] * rscale[:, None, None]
        - hidden_f[:, None, :] * (rscale**3)[:, None, None] * (cross / D)[:, :, None]
    ) * gain
    own_streams, rscale = (
        jnp.concatenate([primal[:, None], tangent], axis=1).astype(jnp.bfloat16),
        rscale,
    )
    streams = lax.all_gather(own_streams, "row", axis=0, tiled=True)
    piece = streams.reshape(tokens * width_s, width_col)
    gate_part = jnp.dot(piece, gate_weight, preferred_element_type=jnp.float32)
    up_part = jnp.dot(piece, up_weight, preferred_element_type=jnp.float32)
    gate_up = lax.psum(
        jnp.stack([gate_part, up_part], axis=1)
        .reshape(tokens, width_s, 2, gate_part.shape[1])
        .astype(jnp.bfloat16),
        "col",
    ).astype(jnp.float32)
    gate = gate_up[:, :, 0]
    up = gate_up[:, :, 1]
    act, slope = silu_parts(gate[:, 0])
    up_primal = up[:, 0]
    tangent_hidden = slope[:, None] * gate[:, 1:] * up_primal[:, None] + act[:, None] * up[:, 1:]
    hidden_act = jnp.concatenate([(act * up_primal)[:, None], tangent_hidden], axis=1).astype(
        jnp.bfloat16
    )
    piece = hidden_act.reshape(rows_row * lax.axis_size("row") * width_s, hidden_act.shape[2])
    down = lax.psum_scatter(
        jnp.dot(piece, down_weight, preferred_element_type=jnp.float32)
        .reshape(rows_row * lax.axis_size("row"), width_s, width_col)
        .astype(jnp.bfloat16),
        "row",
        scatter_dimension=0,
        tiled=True,
    ).astype(jnp.float32)
    output = (hidden_f + down[:, 0]).astype(jnp.bfloat16)
    tangent_out = (vectors[None] + down[:, 1:]).astype(jnp.bfloat16)
    position = lax.axis_index("row") * rows_row + lax.iota(jnp.int32, rows_row)
    prompt = position // LEN
    limit = jnp.sum(
        jnp.where(
            prompt[:, None] == lax.iota(jnp.int32, lengths.shape[0])[None, :], lengths[None, :], 0
        ),
        axis=1,
    )
    live = (position % LEN < limit).astype(jnp.bfloat16)
    cotangent = tangent_out * live[:, None, None]
    cot_all = lax.all_gather(cotangent, "row", axis=0, tiled=True)
    piece = cot_all.reshape(tokens * count, width_col)
    product = contract(piece, down_weight, 1, 1)
    back_hidden = lax.psum(
        product.reshape(tokens, count, product.shape[1]).astype(jnp.bfloat16), "col"
    ).astype(jnp.float32)
    back_gate = (back_hidden * up_primal[:, None] * slope[:, None]).astype(jnp.bfloat16)
    back_up = (back_hidden * act[:, None]).astype(jnp.bfloat16)
    gate_piece = back_gate.reshape(rows_row * lax.axis_size("row") * count, back_gate.shape[2])
    up_piece = back_up.reshape(rows_row * lax.axis_size("row") * count, back_up.shape[2])
    summed = contract(gate_piece, gate_weight, 1, 1) + contract(up_piece, up_weight, 1, 1)
    back_normed = lax.psum_scatter(
        summed.reshape(rows_row * lax.axis_size("row"), count, width_col).astype(jnp.bfloat16),
        "row",
        scatter_dimension=0,
        tiled=True,
    ).astype(jnp.float32)
    scaled = back_normed * gain
    back_cross = lax.psum(jnp.sum(scaled * hidden_f[:, None], axis=2), "col")
    grad = (
        cotangent.astype(jnp.float32)
        + scaled * rscale[:, None, None]
        - hidden_f[:, None] * (rscale**3)[:, None, None] * (back_cross / D)[:, :, None]
    )
    total = lax.psum(jnp.sum(grad, axis=0), "row")
    gram = lax.psum(jnp.dot(total, total.T, precision=HIGH), "col")
    lower = jnp.linalg.cholesky(gram)
    new_vectors = lax.linalg.triangular_solve(lower, total, left_side=True, lower=True) * D**0.5
    return (output, tangent_out, new_vectors, back_cross)


def solution(mesh):
    return jax.shard_map(
        per_device,
        mesh=mesh,
        in_specs=(
            P("row", "col"),
            P(None, "col"),
            P("col"),
            P(),
            P("col", "row"),
            P("col", "row"),
            P("row", "col"),
        ),
        out_specs=(P("row", "col"), P("row", None, "col"), P(None, "col"), P("row", None)),
        check_vma=False,
    )
```

profile of v0, /device:TPU:0, one launch (start us, length us, event | category | flops | bytes accessed | tf_op | source)
XLA Modules:
  0.0 1221.2 jit_solution(5948669985163783054)
XLA Ops:
  9.1 23.2 %all-reduce = (f32[32,4]{0,1:T(4,128)S(1)}, f32[32]{0:T(128)S(1)}) all-reduce(f32[32,4]{0,1:T(4,128)S(1)} %fusion.49, f32[32]{0:T(128)S(1)} %multiply_reduce_fusion.1), channel_id=1, replica_groups=mesh['row'=4,'col'=8] {'col'}, use_global_device_ids=true, to_apply=%region_2.0 | all-reduce | flops 160 | bytes 1280 | tf_op jit(solution)/shard_map/psum | solution.py:32
  35.7 15.5 %all-gather.3.cloned.1.call-done = bf16[128,5,1024]{2,0,1:T(8,128)(2,1)} async-done(((bf16[32,5,1024]{2,0,1:T(8,128)(2,1)}), bf16[128,5,1024]{2,0,1:T(8,128)(2,1)}) %all-gather.3.cloned.1.call-update) | async-done | bytes 1310736 | tf_op jit(solution)/shard_map/all_gather | solution.py:45
  51.2 16.1 %fusion.23 = bf16[128,5,1,7392]{0,3,1,2:T(8,128)(2,1)S(1)} fusion(bf16[128,5,1024]{2,0,1:T(8,128)(2,1)} %all-gather.3.cloned.1.call-done, bf16[1024,7392]{0,1:T(8,128)(2,1)} %param.12), kind=kOutput, calls=%fused_computation.24 | convolution fusion | flops 9693573120 | bytes 25911296 | tf_op jit(solution)/shard_map/dot_general | solution.py:48
  67.3 14.9 %fusion.26 = bf16[128,5,1,7392]{0,3,1,2:T(8,128)(2,1)S(1)} fusion(bf16[128,5,1024]{2,0,1:T(8,128)(2,1)S(1)} %copy-done.10, bf16[1024,7392]{0,1:T(8,128)(2,1)} %param.11), kind=kOutput, calls=%fused_computation.25 | convolution fusion | flops 9693573120 | bytes 25911296 | tf_op jit(solution)/shard_map/dot_general | solution.py:47
  90.3 570.8 %all-reduce.4.cloned.1.call-done = bf16[128,5,2,7392]{0,3,1,2:T(8,128)(2,1)} async-done(((bf16[128,5,2,7392]{0,3,1,2:T(8,128)(2,1)}), bf16[128,5,2,7392]{0,3,1,2:T(8,128)(2,1)}) %all-reduce.4.cloned.1.call-update) | async-done | bytes 18923536 | tf_op jit(solution)/shard_map/psum | solution.py:49
  661.1 20.5 %convert_element_type.55 = f32[128,5,2,7392]{0,3,1,2:T(8,128)} convert(bf16[128,5,2,7392]{0,3,1,2:T(8,128)(2,1)} %all-reduce.4.cloned.1.call-done) | non-fusion elementwise | flops 9461760 | bytes 56770560 | tf_op jit(solution)/shard_map/convert_element_type | solution.py:54
  681.7 19.7 %slice_bitcast_fusion.1 = (f32[128,5,7392]{0,2,1:T(8,128)S(1)}, f32[128,5,7392]{0,2,1:T(8,128)}) fusion(f32[128,5,2,7392]{0,3,1,2:T(8,128)} %convert_element_type.55), kind=kLoop, calls=%fused_computation.1 | loop fusion | bytes 75694080 | tf_op jit(solution)/shard_map/squeeze | solution.py:55
  706.8 12.4 %fusion.4 = bf16[128,4,7392]{0,2,1:T(8,128)(2,1)} fusion(f32[128,5,7392]{0,2,1:T(8,128)} %get-tuple-element.21, f32[128,5,7392]{0,2,1:T(8,128)S(1)} %get-tuple-element.20, f32[128,7392]{0,1:T(8,128)S(1)} %get-tuple-element.23, f32[128,7392]{0,1:T(8,128)} %get-tuple-element.25, f32[128,7392]{0,1:T(8,128)} %get-tuple-element.24), kind=kLoop, calls=%fused_computation.10 | loop fusion | flops 18923520 | bytes 49201152 | tf_op jit(solution)/shard_map/convert.1
  719.2 16.5 %fusion.33 = bf16[128,5,1024]{2,0,1:T(8,128)(2,1)} fusion(bf16[7392,1024]{1,0:T(8,128)(2,1)} %param.13, bf16[128,4,7392]{0,2,1:T(8,128)(2,1)} %fusion.4, bf16[128,1,7392]{0,2,1:T(8,128)(2,1)S(1)} %get-tuple-element.22), kind=kOutput, calls=%fused_computation.35 | convolution fusion | flops 9694228480 | bytes 25911296 | tf_op jit(solution)/shard_map/dot_general | solution.py:65
  735.9 25.4 %reduce-scatter.3.cloned.1.call-done = bf16[32,5,1024]{2,0,1:T(8,128)(2,1)} async-done(((bf16[128,5,1024]{2,0,1:T(8,128)(2,1)}), bf16[32,5,1024]{2,0,1:T(8,128)(2,1)}) %reduce-scatter.3.cloned.1.call-update) | async-done | bytes 327696 | tf_op jit(solution)/shard_map/reduce_scatter | solution.py:64
  763.3 16.8 %all-gather.5.cloned.1.call-done = bf16[128,4,1024]{2,0,1:T(8,128)(2,1)} async-done(((bf16[32,4,1024]{2,0,1:T(8,128)(2,1)}), bf16[128,4,1024]{2,0,1:T(8,128)(2,1)}) %all-gather.5.cloned.1.call-update) | async-done | bytes 1048592 | tf_op jit(solution)/shard_map/all_gather | solution.py:84
  780.1 13.3 %fusion.20 = bf16[128,4,7392]{0,2,1:T(8,128)(2,1)} fusion(bf16[128,4,1024]{2,0,1:T(8,128)(2,1)} %all-gather.5.cloned.1.call-done, bf16[7392,1024]{1,0:T(8,128)(2,1)} %param.13), kind=kOutput, calls=%fused_computation.23 | convolution fusion | flops 7754858496 | bytes 23756800 | tf_op jit(solution)/shard_map/dot_general | solution.py:20
  793.7 246.9 %all-reduce.6.cloned.1.call-done = bf16[128,4,7392]{0,2,1:T(8,128)(2,1)} async-done(((bf16[128,4,7392]{0,2,1:T(8,128)(2,1)}), bf16[128,4,7392]{0,2,1:T(8,128)(2,1)}) %all-reduce.6.cloned.1.call-update) | async-done | bytes 7569424 | tf_op jit(solution)/shard_map/psum | solution.py:87
  1040.6 12.2 fusion.2
  1052.8 13.8 %copy.22 = bf16[128,4,7392]{2,1,0:T(4,128)(2,1)} copy(bf16[128,4,7392]{0,2,1:T(8,128)(2,1)} %get-tuple-element.27) | data formatting | bytes 15138816 | tf_op jit(solution)/shard_map/convert_element_type | solution.py:90
  1066.6 12.3 %reshape.105 = bf16[512,7392]{1,0:T(8,128)(2,1)} reshape(bf16[128,4,7392]{2,1,0:T(4,128)(2,1)} %copy.22) | data formatting | bytes 15138816 | tf_op jit(solution)/shard_map/reshape | solution.py:92
  1078.9 14.5 %fusion.50 = f32[512,1024]{1,0:T(8,128)} fusion(bf16[512,7392]{1,0:T(8,128)(2,1)} %reshape.105, bf16[1024,7392]{0,1:T(8,128)(2,1)} %param.11), kind=kOutput, calls=%fused_computation.77 | convolution fusion | flops 7751073792 | bytes 24805376 | tf_op jit(solution)/shard_map/dot_general | solution.py:20
  1093.4 13.8 %copy.23 = bf16[128,4,7392]{2,1,0:T(4,128)(2,1)} copy(bf16[128,4,7392]{0,2,1:T(8,128)(2,1)} %get-tuple-element.26) | data formatting | bytes 15138816 | tf_op jit(solution)/shard_map/convert_element_type | solution.py:91
  1107.2 12.3 %reshape.106 = bf16[512,7392]{1,0:T(8,128)(2,1)} reshape(bf16[128,4,7392]{2,1,0:T(4,128)(2,1)} %copy.23) | data formatting | bytes 15138816 | tf_op jit(solution)/shard_map/reshape | solution.py:93
  1119.5 13.9 %add_convert_fusion = bf16[512,1024]{1,0:T(8,128)(2,1)S(1)} fusion(f32[512,1024]{1,0:T(8,128)} %fusion.50, bf16[512,7392]{1,0:T(8,128)(2,1)} %reshape.106, bf16[1024,7392]{0,1:T(8,128)(2,1)} %param.12), kind=kOutput, calls=%fused_computation.34 | convolution fusion | flops 7752122368 | bytes 25853952 | tf_op jit(solution)/shard_map/dot_general | solution.py:20
  1135.8 23.3 %reduce-scatter.5.cloned.1.call-done = bf16[32,4,1024]{2,0,1:T(8,128)(2,1)} async-done(((bf16[128,4,1024]{2,0,1:T(8,128)(2,1)}), bf16[32,4,1024]{2,0,1:T(8,128)(2,1)}) %reduce-scatter.5.cloned.1.call-update) | async-done | bytes 262160 | tf_op jit(solution)/shard_map/reduce_scatter | solution.py:95
  1160.3 21.4 %psum.53 = f32[32,4]{0,1:T(4,128)S(1)} all-reduce(f32[32,4]{0,1:T(4,128)S(1)} %multiply_reduce_fusion), channel_id=1, replica_groups=mesh['row'=4,'col'=8] {'col'}, use_global_device_ids=true, to_apply=%region_9.10 | all-reduce | flops 128 | bytes 1024 | tf_op jit(solution)/shard_map/psum | solution.py:102
  1182.9 10.2 psum.54
  1194.2 17.1 %psum.55 = f32[4,4]{0,1:T(4,128)S(1)} all-reduce(f32[4,4]{0,1:T(4,128)S(1)} %fusion.51), channel_id=1, replica_groups=mesh['row'=4,'col'=8] {'col'}, use_global_device_ids=true, to_apply=%region_12.13 | all-reduce | flops 16 | bytes 128 | tf_op jit(solution)/shard_map/psum | solution.py:109
  (67 shorter events, 29.9 us)
Async XLA Ops:
  7.2 44.0 %all-gather.3.cloned.1.call-start = ((), (), s32[]{:S(2)}) async-start(), calls=%async_computation.2 | async-start | bytes 1638400 | tf_op jit(solution)/shard_map/all_gather | solution.py:45
  32.3 2.5 copy-start.8
  33.3 0.7 copy-start.3
  35.6 625.5 %all-reduce.4.cloned.1.call-start = ((), (), s32[]{:S(2)}) async-start(), calls=%async_computation.3 | async-start | bytes 37847040 | tf_op jit(solution)/shard_map/psum | solution.py:49
  51.2 16.1 %copy-start.10 = (bf16[128,5,1024]{2,0,1:T(8,128)(2,1)S(1)}, bf16[128,5,1024]{2,0,1:T(8,128)(2,1)}, u32[]{:S(2)}) copy-start(bf16[128,5,1024]{2,0,1:T(8,128)(2,1)} %all-gather.3.cloned.1.call-done) | copy-start | bytes 3932164
  90.1 671.3 %reduce-scatter.3.cloned.1.call-start = ((), (), s32[]{:S(2)}) async-start(), calls=%async_computation.4 | async-start | bytes 1638400 | tf_op jit(solution)/shard_map/reduce_scatter | solution.py:64
  706.8 12.4 %copy-start = (f32[128,7392]{0,1:T(8,128)}, f32[128,7392]{0,1:T(8,128)S(1)}, u32[]{:S(2)}) copy-start(f32[128,7392]{0,1:T(8,128)S(1)} %get-tuple-element.23) | copy-start | bytes 11354116
  719.2 16.6 %copy-start.11 = (s32[2]{0:T(128)S(1)}, s32[2]{0:T(128)}, u32[]{:S(2)}) copy-start(s32[2]{0:T(128)} %param.10) | copy-start | bytes 28
  719.2 43.2 %copy-start.5 = (f32[4,1024]{1,0:T(4,128)S(1)}, f32[4,1024]{1,0:T(4,128)}, u32[]{:S(2)}) copy-start(f32[4,1024]{1,0:T(4,128)} %param.8) | copy-start | bytes 49156
  735.7 44.4 %all-gather.5.cloned.1.call-start = ((), (), s32[]{:S(2)}) async-start(), calls=%async_computation.5 | async-start | bytes 1310720 | tf_op jit(solution)/shard_map/all_gather | solution.py:84
  763.3 277.4 %all-reduce.6.cloned.1.call-start = ((), (), s32[]{:S(2)}) async-start(), calls=%async_computation.6 | async-start | bytes 15138816 | tf_op jit(solution)/shard_map/psum | solution.py:87
  793.4 365.8 %reduce-scatter.5.cloned.1.call-start = ((), (), s32[]{:S(2)}) async-start(), calls=%async_computation.7 | async-start | bytes 1310720 | tf_op jit(solution)/shard_map/reduce_scatter | solution.py:95
  1119.5 15.7 %copy-start.2 = (bf16[32,1024]{1,0:T(8,128)(2,1)S(1)}, bf16[32,1024]{1,0:T(8,128)(2,1)}, u32[]{:S(2)}) copy-start(bf16[32,1024]{1,0:T(8,128)(2,1)} %param.7) | copy-start | bytes 196612
  1119.5 39.7 %copy-start.6 = (f32[1024]{0:T(1024)S(1)}, f32[1024]{0:T(1024)}, u32[]{:S(2)}) copy-start(f32[1024]{0:T(1024)} %param.9) | copy-start | bytes 12292
  1119.5 62.2 %copy-start.1 = (bf16[32,4,1024]{2,0,1:T(8,128)(2,1)S(1)}, bf16[32,4,1024]{2,0,1:T(8,128)(2,1)}, u32[]{:S(2)}) copy-start(bf16[32,4,1024]{2,0,1:T(8,128)(2,1)} %get-tuple-element.18) | copy-start | bytes 786436
  1119.5 62.2 %copy-start.4 = (f32[32,1024]{1,0:T(8,128)S(1)}, f32[32,1024]{1,0:T(8,128)}, u32[]{:S(2)}) copy-start(f32[32,1024]{1,0:T(8,128)} %copy-done.3) | copy-start | bytes 393220
  1119.5 62.2 %copy-start.9 = (f32[32]{0:T(128)S(1)}, f32[32]{0:T(128)}, u32[]{:S(2)}) copy-start(f32[32]{0:T(128)} %copy-done.8) | copy-start | bytes 388
  1181.7 32.7 %copy-start.7 = (f32[32,4]{0,1:T(4,128)}, f32[32,4]{0,1:T(4,128)S(1)}, u32[]{:S(2)}) copy-start(f32[32,4]{0,1:T(4,128)S(1)} %psum.53) | copy-start | bytes 1540
Sparse Core Ops, SparseCore 0:
  35.8 15.4 all-gather.2
  90.2 570.8 all-reduce.3
  735.9 25.4 reduce-scatter.2
  763.4 16.7 all-gather.4
  793.6 247.0 all-reduce.5
  1135.3 23.8 reduce-scatter.4
where the time goes:
time: 1220 us
  waiting for transfers between devices  899 us (74%)
  matrix products  91.1 us (7%)
  local copies, waits for them, and re-layouts  75.4 us (6%)
  blocking collectives  71.9 us (6%)
  other arithmetic  68.8 us (6%)
  between operations  14.3 us (1%)
    psum x1, waiting for transfers between devices, per_device(): lax.psum(jnp.stack([gate_part, up_part], axis=1).reshape(tokens, width_s,...  571 us
    psum x1, waiting for transfers between devices, per_device(): lax.psum(product.reshape(tokens, count, product.shape[1]).astype(jnp.bflo...  247 us
    dot_general x3, matrix products, contract(): lax.dot_general(left, right, (((left_dim,), (right_dim,)), ((), ())), pre...  41.7 us
    reduce_scatter x1, waiting for transfers between devices, per_device(): lax.psum_scatter(jnp.dot(piece, down_weight, preferred_element_type=jnp.f...  25.4 us
  transfers between devices with their start and end apart: 6, of which 6 were waited for; matrix products, arithmetic and copies ran while one was open for 0% of the time, Pallas kernels for 0%

commit v1 on v0

v1 whole, which is shorter than its diff:
```python
import jax
import jax.numpy as jnp
from jax import lax
from jax.sharding import PartitionSpec as P

D = 8192
LEN = 64


EPSILON = 1e-06
HIGH = lax.Precision.HIGHEST


def silu_parts(value):
    sigmoid = jax.nn.sigmoid(value)
    return (value * sigmoid, sigmoid * (1.0 + value * (1.0 - sigmoid)))


def contract(left, right, left_dim, right_dim):
    return lax.dot_general(
        left, right, (((left_dim,), (right_dim,)), ((), ())), preferred_element_type=jnp.float32
    )


def per_device(hidden, vectors, gain, lengths, gate_weight, up_weight, down_weight):
    rows = hidden.shape[0]
    width = hidden.shape[1]
    count = vectors.shape[0]
    tokens = rows * lax.axis_size("row")
    hidden_all = lax.all_gather(hidden, "row", axis=0, tiled=True)
    hidden_f = hidden_all.astype(jnp.float32)
    sums = lax.psum(
        jnp.concatenate(
            [
                jnp.sum(hidden_f * hidden_f, axis=1)[:, None],
                jnp.dot(hidden_f, vectors.T, precision=HIGH),
            ],
            axis=1,
        ),
        "col",
    )
    rscale = lax.rsqrt(sums[:, 0] / D + EPSILON)
    mix = (rscale**2)[:, None] * sums[:, 1:] / D
    piece = jnp.concatenate([hidden_f * gain, vectors * gain], axis=0).astype(jnp.bfloat16)
    gate_part = jnp.dot(piece, gate_weight, preferred_element_type=jnp.float32)
    up_part = jnp.dot(piece, up_weight, preferred_element_type=jnp.float32)
    gate_up = lax.psum(
        jnp.concatenate([gate_part.astype(jnp.bfloat16), up_part.astype(jnp.bfloat16)], axis=0),
        "col",
    ).astype(jnp.float32)
    high = tokens + count
    gate_raw = gate_up[:tokens]
    gate_vec = gate_up[tokens:high]
    up_raw = gate_up[high : high + tokens]
    up_vec = gate_up[high + tokens :]
    gate = gate_raw * rscale[:, None]
    up = up_raw * rscale[:, None]
    act, slope = silu_parts(gate)
    slope_up = slope * up
    scaled_act = act * rscale[:, None]
    scaled_slope = slope_up * rscale[:, None]
    both = slope_up * gate + act * up
    tangent_hidden = (
        scaled_slope[None] * gate_vec[:, None]
        + scaled_act[None] * up_vec[:, None]
        - mix.T[:, :, None] * both[None]
    )
    hidden_act = jnp.concatenate([(act * up)[None], tangent_hidden], axis=0).astype(jnp.bfloat16)
    down = lax.psum_scatter(
        jnp.dot(
            hidden_act.reshape((count + 1) * tokens, -1),
            down_weight,
            preferred_element_type=jnp.float32,
        )
        .reshape(count + 1, tokens, width)
        .astype(jnp.bfloat16),
        "row",
        scatter_dimension=1,
        tiled=True,
    ).astype(jnp.float32)
    output = (hidden.astype(jnp.float32) + down[0]).astype(jnp.bfloat16)
    tangent = (vectors[:, None] + down[1:]).astype(jnp.bfloat16)
    start = lax.axis_index("row") * rows
    position = start + lax.iota(jnp.int32, rows)
    prompt = position // LEN
    limit = jnp.sum(
        jnp.where(
            prompt[:, None] == lax.iota(jnp.int32, lengths.shape[0])[None, :], lengths[None, :], 0
        ),
        axis=1,
    )
    live = (position % LEN < limit).astype(jnp.bfloat16)
    cotangent = tangent * live[None, :, None]
    cot_all = lax.all_gather(cotangent, "row", axis=1, tiled=True)
    product = contract(cot_all.reshape(count * tokens, width), down_weight, 1, 1).reshape(
        count, tokens, -1
    )
    gate_sum = jnp.sum(product * scaled_slope[None], axis=1)
    up_sum = jnp.sum(product * scaled_act[None], axis=1)
    weight = slope_up * gate_raw + act * up_raw
    cross_part = jnp.sum(product * weight[None], axis=2)
    gate_sum, up_sum, cross_part = lax.psum((gate_sum, up_sum, cross_part), "col")
    pulled = gain * (
        contract(gate_sum.astype(jnp.bfloat16), gate_weight, 1, 1)
        + contract(up_sum.astype(jnp.bfloat16), up_weight, 1, 1)
    )
    shift = jnp.dot(cross_part * (rscale**3 / D)[None, :], hidden_f, precision=HIGH)
    partial = jnp.sum(cotangent.astype(jnp.float32), axis=1) + pulled - shift
    total, back_cross = lax.psum((partial, cross_part), "row")
    gram = lax.psum(jnp.dot(total, total.T, precision=HIGH), "col")
    lower = jnp.linalg.cholesky(gram)
    new_vectors = lax.linalg.triangular_solve(lower, total, left_side=True, lower=True) * D**0.5
    own_cross = lax.dynamic_slice_in_dim(back_cross, start, rows, axis=1).T
    return (output, jnp.transpose(tangent, (1, 0, 2)), new_vectors, own_cross)


def solution(mesh):
    return jax.shard_map(
        per_device,
        mesh=mesh,
        in_specs=(
            P("row", "col"),
            P(None, "col"),
            P("col"),
            P(),
            P("col", "row"),
            P("col", "row"),
            P("row", "col"),
        ),
        out_specs=(P("row", "col"), P("row", None, "col"), P(None, "col"), P("row", None)),
        check_vma=False,
    )
```

time: 1220 us -> 447 us (0.37)
  waiting for transfers between devices: 899 us -> 215 us
  local copies, waits for them, and re-layouts: 75.4 us -> 13.5 us
  other arithmetic: 68.8 us -> 39.8 us
  blocking collectives: 71.9 us -> 98.3 us
  matrix products: 91.1 us -> 66.2 us
    psum x2 -> x1, waiting for transfers between devices: 818 us -> 173 us  [per_device(): lax.psum(jnp.concatenate([gate_part.astype(jnp.bfloat16), up_part.astype(...]
    convert_element_type x5 -> x3, other arithmetic: 34.4 us -> 5.04 us  [the longest x1 3.36 us: per_device(): gate_up = lax.psum(jnp.concatenate([gate_part.astype(jnp.bfloat16), up_pa...]
    convert_element_type x4 -> x0, local copies, waits for them, and re-layouts: 29.3 us -> none  [the longest x1 13.8 us: per_device(): (back_hidden * up_primal[:, None] * slope[:, None]).astype(jnp.bfloat16)]
    reshape x2 -> x0, local copies, waits for them, and re-layouts: 24.6 us -> none  [the longest x1 12.3 us: per_device(): back_up.reshape(rows_row * lax.axis_size('row') * count, back_up.shape[2])]
    reduce_scatter x2 -> x1, waiting for transfers between devices: 48.8 us -> 25.2 us  [per_device(): lax.psum_scatter(jnp.dot(hidden_act.reshape((count + 1) * tokens, -1), do...]
    squeeze x1 -> x0, local copies, waits for them, and re-layouts: 19.7 us -> none  [per_device(): gate = gate_up[:, :, 0]]
    psum x3, blocking collectives: 54.8 us -> 73.7 us  [the longest x1 40.5 us: per_device(): lax.psum((gate_sum, up_sum, cross_part), 'col')]
    all_gather x2 -> x1, waiting for transfers between devices: 32.3 us -> 16.3 us  [per_device(): cot_all = lax.all_gather(cotangent, 'row', axis=1, tiled=True)]
  transfers between devices with their start and end apart: 6 -> 3, of which waited for: 6 -> 3; matrix products, arithmetic and copies ran while one was open for 0% -> 0% of each run, Pallas kernels for 0% -> 0%
where the time goes in v1:
time: 447 us
  waiting for transfers between devices  215 us (48%)
  blocking collectives  98.3 us (22%)
  matrix products  66.2 us (15%)
  other arithmetic  39.8 us (9%)
  between operations  14 us (3%)
  local copies, waits for them, and re-layouts  13.5 us (3%)
    psum x1, waiting for transfers between devices, per_device(): lax.psum(jnp.concatenate([gate_part.astype(jnp.bfloat16), up_part.astype(...  173 us
    psum x1, blocking collectives, per_device(): lax.psum((gate_sum, up_sum, cross_part), 'col')  40.5 us
    dot_general x3, matrix products, contract(): lax.dot_general(left, right, (((left_dim,), (right_dim,)), ((), ())), pre...  34.9 us
    reduce_scatter x1, waiting for transfers between devices, per_device(): lax.psum_scatter(jnp.dot(hidden_act.reshape((count + 1) * tokens, -1), do...  25.2 us
    psum x1, blocking collectives, per_device(): lax.psum(jnp.concatenate([jnp.sum(hidden_f * hidden_f, axis=1)[:, None],...  22.9 us
    psum x1, blocking collectives, per_device(): gram = lax.psum(jnp.dot(total, total.T, precision=HIGH), 'col')  17.1 us
    all_gather x1, waiting for transfers between devices, per_device(): cot_all = lax.all_gather(cotangent, 'row', axis=1, tiled=True)  16.3 us
    dot_general x1, matrix products, per_device(): jnp.dot(hidden_act.reshape((count + 1) * tokens, -1), down_weight, prefer...  14.4 us
  transfers between devices with their start and end apart: 3, of which 3 were waited for; matrix products, arithmetic and copies ran while one was open for 0% of the time, Pallas kernels for 0%

profile of v1, /device:TPU:0, one launch (start us, length us, event | category | flops | bytes accessed | tf_op | source)
XLA Modules:
  0.0 446.8 jit_solution(3471435014731667358)
XLA Ops:
  7.2 7.4 %all_gather.6 = bf16[128,1024]{1,0:T(8,128)(2,1)S(1)} all-gather(bf16[32,1024]{1,0:T(8,128)(2,1)} %param.7), channel_id=1, replica_groups=mesh['row'=4,'col'=8] {'row'}, dimensions={0}, use_global_device_ids=true | all-gather | bytes 327680 | tf_op jit(solution)/shard_map/all_gather | solution.py:30
  16.2 9.6 %convolution_convert_fusion = bf16[132,7392]{0,1:T(8,128)(2,1)S(1)} fusion(bf16[1024,7392]{0,1:T(8,128)(2,1)} %param.12, bf16[4,1024]{1,0:T(4,128)(2,1)S(1)} %multiply_convert_fusion, bf16[128,1024]{1,0:T(8,128)(2,1)S(1)} %get-tuple-element.40), kind=kOutput, calls=%fused_computation.8 | convolution fusion | flops 1999840128 | bytes 17360640 | tf_op jit(solution)/shard_map/dot_general | solution.py:46
  25.8 5.9 %convolution_convert_fusion.1 = bf16[132,7392]{0,1:T(8,128)(2,1)} fusion(bf16[1024,7392]{0,1:T(8,128)(2,1)S(1)} %copy-done.2, bf16[4,1024]{1,0:T(4,128)(2,1)S(1)} %multiply_convert_fusion, bf16[128,1024]{1,0:T(8,128)(2,1)S(1)} %get-tuple-element.40), kind=kOutput, calls=%fused_computation.9 | convolution fusion | flops 1999840128 | bytes 17360640 | tf_op jit(solution)/shard_map/dot_general | solution.py:45
  31.7 6.8 %pad_maximum_fusion = bf16[264,7392]{0,1:T(8,128)(2,1)} fusion(bf16[132,7392]{0,1:T(8,128)(2,1)S(1)} %convolution_convert_fusion, bf16[132,7392]{0,1:T(8,128)(2,1)} %convolution_convert_fusion.1), kind=kLoop, calls=%fused_computation.13 | loop fusion | flops 7805952 | bytes 7805952 | tf_op jit(solution)/shard_map/concatenate | solution.py:48
  39.5 22.9 %psum.57 = f32[128,5]{0,1:T(8,128)S(1)} all-reduce(f32[128,5]{0,1:T(8,128)S(1)} %pad_maximum_fusion.4), channel_id=1, replica_groups=mesh['row'=4,'col'=8] {'col'}, use_global_device_ids=true, to_apply=%region_2.0 | all-reduce | flops 640 | bytes 5120 | tf_op jit(solution)/shard_map/psum | solution.py:32
  62.5 173.1 %all-reduce.5.cloned.1.call-done = bf16[264,7392]{0,1:T(8,128)(2,1)} async-done(((bf16[264,7392]{0,1:T(8,128)(2,1)}), bf16[264,7392]{0,1:T(8,128)(2,1)}) %all-reduce.5.cloned.1.call-update) | async-done | bytes 3902992 | tf_op jit(solution)/shard_map/psum | solution.py:47
  235.5 5.7 %fusion.35 = (f32[4,7392]{0,1:T(8,128)}, f32[4,7392]{0,1:T(8,128)}) fusion(bf16[264,7392]{0,1:T(8,128)(2,1)} %all-reduce.5.cloned.1.call-done), kind=kLoop, calls=%fused_computation.78 | loop fusion | bytes 473088 | tf_op jit(solution)/shard_map/slice | solution.py:53
  241.2 2.7 copy.31
  243.9 2.7 copy.32
  246.6 3.4 convert_element_type.51
  250.0 4.9 %convert_bitcast_fusion = (bf16[1,128,7392]{1,2,0:T(8,128)(2,1)}, f32[128,7392]{0,1:T(8,128)S(1)}, f32[128,7392]{0,1:T(8,128)}, f32[128,7392]{0,1:T(8,128)}) fusion(f32[128]{0:T(128)S(1)} %bitcast.53, f32[264,7392]{0,1:T(8,128)S(1)} %convert_element_type.51), kind=kLoop, calls=%fused_computation.22 | loop fusion | flops 16084992 | bytes 20816384 | tf_op jit(solution)/shard_map/broadcast_in_dim | solution.py:68
  254.9 5.9 %broadcast_multiply_fusion.1 = (f32[128,7392]{0,1:T(8,128)S(1)}, f32[128,7392]{0,1:T(8,128)}) fusion(f32[128,7392]{0,1:T(8,128)} %get-tuple-element.33, f32[128]{0:T(128)S(1)} %bitcast.54, f32[264,7392]{0,1:T(8,128)S(1)} %convert_element_type.51), kind=kLoop, calls=%fused_computation.24 | loop fusion | flops 9461760 | bytes 18924032 | tf_op jit(solution)/shard_map/mul | solution.py:61
  260.8 12.7 %subtract_convert_fusion = bf16[4,128,7392]{1,2,0:T(8,128)(2,1)} fusion(f32[128,7392]{0,1:T(8,128)} %get-tuple-element.37, f32[4,128]{1,0:T(4,128)S(1)} %multiply_bitcast_fusion, f32[4,7392]{1,0:T(4,128)S(1)} %copy.32, f32[128,7392]{0,1:T(8,128)S(1)} %get-tuple-element.31, f32[4,7392]{1,0:T(4,128)S(1)} %copy.31, f32[128,7392]{0,1:T(8,128)S(1)} %get-tuple-element.36), kind=kLoop, calls=%fused_computation.7 | loop fusion | flops 22708224 | bytes 19162112 | tf_op jit(solution)/shard_map/convert.1
  273.5 14.4 %fusion.9 = bf16[5,128,1024]{2,1,0:T(8,128)(2,1)} fusion(bf16[7392,1024]{1,0:T(8,128)(2,1)S(1)} %bitcast.52, bf16[4,128,7392]{1,2,0:T(8,128)(2,1)} %subtract_convert_fusion, bf16[1,128,7392]{1,2,0:T(8,128)(2,1)} %get-tuple-element.30), kind=kOutput, calls=%fused_computation.25 | convolution fusion | flops 9694228480 | bytes 25911296 | tf_op jit(solution)/shard_map/dot_general | solution.py:70
  288.4 25.2 %reduce-scatter.2.cloned.1.call-done = bf16[5,32,1024]{2,1,0:T(8,128)(2,1)} async-done(((bf16[5,128,1024]{2,1,0:T(8,128)(2,1)}), bf16[5,32,1024]{2,1,0:T(8,128)(2,1)}) %reduce-scatter.2.cloned.1.call-update) | async-done | bytes 327696 | tf_op jit(solution)/shard_map/reduce_scatter | solution.py:69
  313.6 1.0 convert_element_type.53
  316.1 16.3 %all-gather.2.cloned.1.call-done = bf16[4,128,1024]{2,1,0:T(8,128)(2,1)} async-done(((bf16[4,32,1024]{2,1,0:T(8,128)(2,1)}), bf16[4,128,1024]{2,1,0:T(8,128)(2,1)}) %all-gather.2.cloned.1.call-update) | async-done | bytes 1048592 | tf_op jit(solution)/shard_map/all_gather | solution.py:94
  332.4 20.1 %multiply_reduce_fusion = (f32[4,128]{1,0:T(4,128)S(1)}, f32[4,7392]{1,0:T(4,128)S(1)}, f32[4,7392]{1,0:T(4,128)S(1)}) fusion(f32[128,7392]{0,1:T(8,128)} %get-tuple-element.32, f32[128,7392]{0,1:T(8,128)} %copy-done, f32[128,7392]{0,1:T(8,128)} %copy-done.1, bf16[4,128,1024]{2,1,0:T(8,128)(2,1)} %all-gather.2.cloned.1.call-done, bf16[7392,1024]{1,0:T(8,128)(2,1)} %param.13), kind=kOutput, calls=%fused_computation.4 | convolution fusion | flops 7773722112 | bytes 27780096 | tf_op jit(solution)/shard_map/dot_general | solution.py:20
  352.6 40.5 %all-reduce.6 = (bf16[4,7392]{1,0:T(4,128)(2,1)S(1)}, bf16[4,7392]{1,0:T(4,128)(2,1)S(1)}, f32[4,128]{1,0:T(4,128)S(1)}) all-reduce(f32[4,7392]{1,0:T(4,128)S(1)} %get-tuple-element.18, f32[4,7392]{1,0:T(4,128)S(1)} %get-tuple-element.17, f32[4,128]{1,0:T(4,128)S(1)} %get-tuple-element.16), channel_id=1, replica_groups=mesh['row'=4,'col'=8] {'col'}, use_global_device_ids=true, to_apply=%region_7.8 | all-reduce | flops 59648 | bytes 358912 | tf_op jit(solution)/shard_map/psum | solution.py:102
  393.1 7.4 %fusion.38 = f32[4,1024]{1,0:T(4,128)S(1)} fusion(bf16[4,7392]{1,0:T(4,128)(2,1)S(1)} %get-tuple-element.19, bf16[1024,7392]{0,1:T(8,128)(2,1)} %param.11), kind=kOutput, calls=%fused_computation.81 | convolution fusion | flops 60555264 | bytes 15214336 | tf_op jit(solution)/shard_map/dot_general | solution.py:20
  400.5 7.4 %fusion.15 = f32[4,1024]{1,0:T(4,128)S(1)} fusion(f32[4,1024]{1,0:T(4,128)S(1)} %get-tuple-element.28, f32[4,1024]{1,0:T(4,128)S(1)} %fusion.38, bf16[1024,7392]{0,1:T(8,128)(2,1)} %param.12, bf16[4,7392]{1,0:T(4,128)(2,1)S(1)} %get-tuple-element.20, f32[1024]{0:T(1024)S(1)} %copy-done.5), kind=kOutput, calls=%fused_computation.30 | convolution fusion | flops 60567552 | bytes 15251200 | tf_op jit(solution)/shard_map/dot_general | solution.py:20
  408.1 10.3 %all-reduce.1 = (f32[4,1024]{1,0:T(4,128)S(1)}, f32[4,128]{1,0:T(4,128)S(1)}) all-reduce(f32[4,1024]{1,0:T(4,128)S(1)} %convolution_subtract_fusion, f32[4,128]{1,0:T(4,128)S(1)} %get-tuple-element.21), channel_id=1, replica_groups=mesh['row'=4,'col'=8] {'row'}, use_global_device_ids=true, to_apply=%region_12.13 | all-reduce | flops 4608 | bytes 36864 | tf_op jit(solution)/shard_map/psum | solution.py:109
  418.6 0.9 copy.36
  419.5 17.1 %psum.62 = f32[4,4]{0,1:T(4,128)S(1)} all-reduce(f32[4,4]{0,1:T(4,128)S(1)} %fusion.37), channel_id=1, replica_groups=mesh['row'=4,'col'=8] {'col'}, use_global_device_ids=true, to_apply=%region_13.14 | all-reduce | flops 16 | bytes 128 | tf_op jit(solution)/shard_map/psum | solution.py:110
  (52 shorter events, 8.6 us)
Async XLA Ops:
  7.2 228.4 %all-reduce.5.cloned.1.call-start = ((), (), s32[]{:S(2)}) async-start(), calls=%async_computation.1 | async-start | bytes 11354112 | tf_op jit(solution)/shard_map/psum | solution.py:47
  16.2 9.6 %copy-start.2 = (bf16[1024,7392]{0,1:T(8,128)(2,1)S(1)}, bf16[1024,7392]{0,1:T(8,128)(2,1)}, u32[]{:S(2)}) copy-start(bf16[1024,7392]{0,1:T(8,128)(2,1)} %param.11) | copy-start | bytes 45416452
  38.5 0.7 copy-start.4
  38.5 275.1 %reduce-scatter.2.cloned.1.call-start = ((), (), s32[]{:S(2)}) async-start(), calls=%async_computation.2 | async-start | bytes 1638400 | tf_op jit(solution)/shard_map/reduce_scatter | solution.py:69
  254.9 5.9 %copy-start = (f32[128,7392]{0,1:T(8,128)}, f32[128,7392]{0,1:T(8,128)S(1)}, u32[]{:S(2)}) copy-start(f32[128,7392]{0,1:T(8,128)S(1)} %get-tuple-element.31) | copy-start | bytes 11354116
  254.9 18.6 %slice-start = ((s8[15138816]{0:T(1024)(128)(4,1)}), s8[2555904]{0:T(1024)(128)(4,1)S(1)}, s32[]{:S(2)}) async-start(s8[15138816]{0:T(1024)(128)(4,1)} %bitcast.51), calls=%async_computation.4 | async-start | bytes 5111808
  254.9 18.6 %slice-start.1 = ((s8[15138816]{0:T(1024)(128)(4,1)}), s8[4194304]{0:T(1024)(128)(4,1)S(1)}, s32[]{:S(2)}) async-start(s8[15138816]{0:T(1024)(128)(4,1)} %bitcast.51), calls=%async_computation.5 | async-start | bytes 8388608
  260.7 12.7 %copy-start.1 = (f32[128,7392]{0,1:T(8,128)}, f32[128,7392]{0,1:T(8,128)S(1)}, u32[]{:S(2)}) copy-start(f32[128,7392]{0,1:T(8,128)S(1)} %get-tuple-element.36) | copy-start | bytes 11354116
  260.7 12.7 %slice-start.2 = ((s8[15138816]{0:T(1024)(128)(4,1)}), s8[4194304]{0:T(1024)(128)(4,1)S(1)}, s32[]{:S(2)}) async-start(s8[15138816]{0:T(1024)(128)(4,1)} %bitcast.51), calls=%async_computation.6 | async-start | bytes 8388608
  260.8 12.7 %slice-start.3 = ((s8[15138816]{0:T(1024)(128)(4,1)}), s8[4194304]{0:T(1024)(128)(4,1)S(1)}, s32[]{:S(2)}) async-start(s8[15138816]{0:T(1024)(128)(4,1)} %bitcast.51), calls=%async_computation.7 | async-start | bytes 8388608
  273.5 14.8 %copy-start.6 = (s32[2]{0:T(128)S(1)}, s32[2]{0:T(128)}, u32[]{:S(2)}) copy-start(s32[2]{0:T(128)} %param.10) | copy-start | bytes 28
  273.5 41.9 %copy-start.3 = (bf16[32,1024]{1,0:T(8,128)(2,1)S(1)}, bf16[32,1024]{1,0:T(8,128)(2,1)}, u32[]{:S(2)}) copy-start(bf16[32,1024]{1,0:T(8,128)(2,1)} %param.7) | copy-start | bytes 196612
  288.0 44.5 %all-gather.2.cloned.1.call-start = ((), (), s32[]{:S(2)}) async-start(), calls=%async_computation.3 | async-start | bytes 1310720 | tf_op jit(solution)/shard_map/all_gather | solution.py:94
  393.1 7.4 %copy-start.5 = (f32[1024]{0:T(1024)S(1)}, f32[1024]{0:T(1024)}, u32[]{:S(2)}) copy-start(f32[1024]{0:T(1024)} %param.9) | copy-start | bytes 12292
Sparse Core Ops, SparseCore 0:
  38.6 196.8 all-reduce.4
  288.1 25.4 reduce-scatter.1
  315.7 16.6 all-gather.1
